TPU v7x, 32 devices: a whole 2x2x4 slice. The times are simulated.
32 devices in a mesh: region: 8 (over z, y), depth: 4 (over x, core).
Axes of the slice: x: 2, y: 2, z: 4, core: 2. Of those that a mesh axis runs over, the one named last changes fastest.
Arguments:
- displacement: float32 [16, 16, 3, 1024], P('depth', None, None, 'region'), may hold values from -1.5 to 1.5
- velocity: float32 [16, 16, 3, 1024], P('depth', None, None, 'region'), may hold values from -4 to 4
- growth: float32 [16, 16, 1024], P('depth', None, 'region'), may hold values from 1 to 1.6
- shear_modulus: float32 [16, 16, 1024], P('depth', None, 'region'), may hold values from 0.3 to 3
- pair_slots: int32 [4, 8, 3, 16], P('depth', 'region'), may hold values from 0 to 63, as said below
- pair_count: int32 [4, 8], P('depth', 'region'), may hold values from 12 to 16, as said below
- separation: float32 [4, 8, 3, 16], P('depth', 'region'), may hold values from -1 to 1, as said below
Outputs:
- new_velocity: float32 [16, 16, 3, 1024], P('depth', None, None, 'region')
- new_displacement: float32 [16, 16, 3, 1024], P('depth', None, None, 'region')
Inputs may be any that keep to these rules, and one draw needn't show every extreme that they name: `pair_slots`: row 0 of a slot is a patch of the own region below 64, row 1 a region, row 2 a patch of that region below 64. Slots k < pair_count[s, r] are live and name another region; the rest hold arbitrary values in the same ranges. Contact is symmetric: a live slot (l, m, q) with separation o on (s, r) comes with a live slot (q, r, l) with separation -o on (s, m). At most 4 live slots of one region and slab name the same region; in every slab some region has exactly 4 live slots for every region it names. `pair_count`: in every slab some region has 16 live slots. `separation`: opposite on the two sides of a contact, as stated for pair_slots.
All inputs are finite; a program needn't handle non-finite values.
Results may differ from a plain program's by a relative error of at most 0.0003.
Values sent between devices are 32-bit elements; how exact they have to be, the bound alone decides.
No kernel may reach another device: no remote copies, remote signals or barrier semaphores. Data moves between devices by JAX's collectives and lax.ppermute only.
A program may use at most 64 MiB of HBM per device.

v0:
```python
import math
import jax
import jax.numpy as jnp
from jax import lax
from jax.sharding import PartitionSpec as P

CAP = 4
PERMUTATIONS = ((0, 1, 2), (0, 2, 1), (1, 0, 2), (1, 2, 0), (2, 0, 1), (2, 1, 0))
CORNER_SET = (
    (0, 0, 0),
    (0, 0, 1),
    (0, 1, 0),
    (0, 1, 1),
    (1, 0, 0),
    (1, 0, 1),
    (1, 1, 0),
    (1, 1, 1),
)
REST_VOLUME = 1.0 / 6.0
STEP_TIME = 0.2


def with_halo(cells, sides, width):
    for axis, dim in sides:
        count = lax.axis_size(axis)
        head = lax.slice_in_dim(cells, 0, width, axis=dim)
        tail = lax.slice_in_dim(cells, cells.shape[dim] - width, cells.shape[dim], axis=dim)
        cells = jnp.concatenate(
            [
                lax.ppermute(tail, axis, [(i, (i + 1) % count) for i in range(count)]),
                cells,
                lax.ppermute(head, axis, [((i + 1) % count, i) for i in range(count)]),
            ],
            axis=dim,
        )
    return cells


def unit_step(component):
    return tuple((1 if position == 2 - component else 0 for position in range(3)))


def joined(first_offset, second_offset):
    return tuple((first_offset[index] + second_offset[index] for index in range(3)))


def shifted(field, offset):
    return jnp.roll(field, (-offset[0], -offset[1], -offset[2]), axis=(0, 1, 2))


def cell_forces(displacement, growth, shear, valid):
    fields = [displacement[:, :, index, :] for index in range(3)]
    corners = {offset: [shifted(field, offset) for field in fields] for offset in CORNER_SET}
    inverse = 1.0 / growth
    squared = growth * growth
    weight = valid * REST_VOLUME
    totals = {offset: [jnp.zeros_like(growth) for index in range(3)] for offset in CORNER_SET}
    for ordering in PERMUTATIONS:
        first_axis, second_axis, third_axis = ordering
        start = (0, 0, 0)
        middle = unit_step(first_axis)
        upper = joined(middle, unit_step(second_axis))
        summit = (1, 1, 1)
        columns = [None, None, None]
        columns[first_axis] = [corners[middle][row] - corners[start][row] for row in range(3)]
        columns[second_axis] = [corners[upper][row] - corners[middle][row] for row in range(3)]
        columns[third_axis] = [corners[summit][row] - corners[upper][row] for row in range(3)]
        elastic_f = [
            [
                (columns[col][row] + (1.0 if row == col else 0.0)) * (inverse if col < 2 else 1.0)
                for col in range(3)
            ]
            for row in range(3)
        ]
        cofactor = [
            [
                elastic_f[(row + 1) % 3][(col + 1) % 3] * elastic_f[(row + 2) % 3][(col + 2) % 3]
                - elastic_f[(row + 1) % 3][(col + 2) % 3] * elastic_f[(row + 2) % 3][(col + 1) % 3]
                for col in range(3)
            ]
            for row in range(3)
        ]
        jacobian = (
            elastic_f[0][0] * cofactor[0][0]
            + elastic_f[0][1] * cofactor[0][1]
            + elastic_f[0][2] * cofactor[0][2]
        )
        pressure = 4.0 * (jacobian - 1.25)
        stress = [
            [
                shear
                * (elastic_f[row][col] + pressure * cofactor[row][col])
                * (growth if col < 2 else squared)
                * weight
                for col in range(3)
            ]
            for row in range(3)
        ]
        for row in range(3):
            col_first = stress[row][first_axis]
            col_second = stress[row][second_axis]
            col_third = stress[row][third_axis]
            totals[start][row] = totals[start][row] + col_first
            totals[middle][row] = totals[middle][row] + (col_second - col_first)
            totals[upper][row] = totals[upper][row] + (col_third - col_second)
            totals[summit][row] = totals[summit][row] - col_third
    result = []
    for row in range(3):
        summed = jnp.zeros_like(growth)
        for offset in CORNER_SET:
            summed = summed + jnp.roll(totals[offset][row], offset, axis=(0, 1, 2))
        result.append(summed)
    return jnp.stack(result, axis=2)


def pair_forces(near, far):
    deltas = [near[:, index, :, None] - far[:, index, None, :] for index in range(3)]
    distance = deltas[0] * deltas[0] + deltas[1] * deltas[1] + deltas[2] * deltas[2]
    kernel = jnp.exp(-distance)
    return jnp.stack([jnp.sum(delta * kernel, axis=2) for delta in deltas], axis=1)


def blocked_forces(near, far):
    total_rows = near.shape[0]
    block = math.gcd(total_rows, 32)
    shaped = (total_rows // block, block) + near.shape[1:]
    result = lax.map(
        lambda couple: pair_forces(couple[0], couple[1]),
        (near.reshape(shaped), far.reshape(shaped)),
    )
    return result.reshape(near.shape)


def local(displacement, velocity, growth, shear_modulus, pair_slots, pair_count, separation):
    slab_len, width_y, _, patch_len = displacement.shape
    regions = lax.axis_size("region")
    slabs = lax.axis_size("depth")
    depth_index = lax.axis_index("depth")
    stacked = jnp.concatenate(
        [displacement, growth[:, :, None, :], shear_modulus[:, :, None, :]], axis=2
    )
    extended = with_halo(stacked, (("region", 3), ("depth", 0)), 1)
    z_local = jnp.arange(slab_len + 2, dtype=jnp.int32)
    z_global = depth_index * slab_len + z_local - 1
    z_valid = (z_local <= slab_len) & (z_global >= 0) & (z_global <= slab_len * slabs - 2)
    y_valid = jnp.arange(width_y, dtype=jnp.int32) <= width_y - 2
    x_valid = jnp.arange(patch_len + 2, dtype=jnp.int32) <= patch_len
    valid = (z_valid[:, None, None] & y_valid[None, :, None] & x_valid[None, None, :]).astype(
        jnp.float32
    )
    elastic_ext = cell_forces(
        extended[:, :, 0:3, :], extended[:, :, 3, :], extended[:, :, 4, :], valid
    )
    elastic = elastic_ext[1 : slab_len + 1, :, :, 1 : patch_len + 1]
    patches_dev = slab_len * width_y
    component_row = lax.broadcasted_iota(jnp.int32, (3, patch_len), 0)
    along_row = lax.broadcasted_iota(jnp.int32, (3, patch_len), 1).astype(jnp.float32)
    rest_line = jnp.where(component_row == 0, along_row, jnp.zeros_like(along_row))
    own_points = displacement.reshape(patches_dev, 3, patch_len) + rest_line
    slots = pair_slots[0, 0]
    own_patch = slots[0]
    peer_region = slots[1]
    peer_patch = slots[2]
    slot_total = slots.shape[1]
    offsets = jnp.transpose(separation[0, 0])
    live = jnp.arange(slot_total, dtype=jnp.int32) < pair_count[0, 0]
    onehot_peer = (
        (peer_region[:, None] == jnp.arange(regions, dtype=jnp.int32)[None, :]) & live[:, None]
    ).astype(jnp.int32)
    before = jnp.cumsum(onehot_peer, axis=0) - onehot_peer
    rank = jnp.sum(before * onehot_peer, axis=1)
    buckets = regions * CAP
    bucket = jnp.where(live, peer_region * CAP + rank, buckets)
    outgoing = (
        jnp.zeros((buckets, 3, patch_len), jnp.float32)
        .at[bucket]
        .set(own_points[own_patch] - offsets[:, :, None], mode="drop")
    )
    labels = (
        jnp.full((buckets,), -1.0, jnp.float32)
        .at[bucket]
        .set(peer_patch.astype(jnp.float32), mode="drop")
    )
    arrived, arrived_labels = (
        lax.all_to_all(
            outgoing.reshape(regions, CAP, 3, patch_len),
            "region",
            split_axis=0,
            concat_axis=0,
            tiled=True,
        ),
        lax.all_to_all(
            labels.reshape(regions, CAP), "region", split_axis=0, concat_axis=0, tiled=True
        ),
    )
    arrived = arrived.reshape(buckets, 3, patch_len)
    arrived_labels = arrived_labels.reshape(buckets)
    chosen = arrived_labels >= 0.0
    targets = jnp.where(chosen, arrived_labels, 0.0).astype(jnp.int32)
    forces = blocked_forces(own_points[targets], arrived) * chosen[:, None, None].astype(
        jnp.float32
    )
    selector = (
        (targets[:, None] == jnp.arange(patches_dev, dtype=jnp.int32)[None, :]) & chosen[:, None]
    ).astype(jnp.float32)
    contact = jnp.einsum("kp,kcx->pcx", selector, forces, precision=lax.Precision.HIGHEST)
    contact = contact.reshape(slab_len, width_y, 3, patch_len)
    new_velocity = velocity + STEP_TIME * (elastic + contact)
    new_displacement = displacement + STEP_TIME * new_velocity
    return (new_velocity, new_displacement)


def solution(mesh):
    in_specs = (
        P("depth", None, None, "region"),
        P("depth", None, None, "region"),
        P("depth", None, "region"),
        P("depth", None, "region"),
        P("depth", "region", None, None),
        P("depth", "region"),
        P("depth", "region", None, None),
    )
    out_specs = (P("depth", None, None, "region"), P("depth", None, None, "region"))
    return jax.shard_map(local, mesh=mesh, in_specs=in_specs, out_specs=out_specs, check_vma=False)
```

profile of v0, /device:TPU:1, one launch (start us, length us, event | category | flops | bytes accessed | tf_op | source)
XLA Modules:
  0.0 50.1 jit_solution(1736963173095069045)
XLA Ops:
  1.3 0.7 %convert_bitcast_fusion = (f32[16]{0:T(128)S(1)}, s32[16]{0:T(128)S(1)}) fusion(s32[1,1,3,16]{3,1,2,0:T(1,128)} %param.11), kind=kLoop, calls=%fused_computation.623 | loop fusion | flops 16 | bytes 256 | tf_op jit(solution)/shard_map/convert_element_type | solution.py:182
  2.1 0.2 select_reduce_fusion
  2.3 0.7 %fusion.163 = (s32[16]{0:T(128)S(1)}, s32[16]{0:T(128)S(1)}) fusion(s32[1,1,3,16]{3,1,2,0:T(1,128)} %param.11, s32[16]{0:T(128)S(1)} %select_reduce_fusion, s32[]{:T(128)} %bitcast.952), kind=kLoop, calls=%fused_computation.618 | loop fusion | flops 160 | bytes 324 | tf_op jit(solution)/shard_map/select_n | solution.py:177
  2.9 0.6 %scatter_custom_fusion = f32[32]{0:T(128)S(1)} fusion(s32[16]{0:T(128)S(1)} %get-tuple-element.149, f32[16]{0:T(128)S(1)} %get-tuple-element.146, f32[]{:T(128)} %constant.30.clone.1), kind=kCustom, calls=%fused_computation.629 | custom fusion | bytes 132 | tf_op jit(solution)/shard_map/scatter | solution.py:182
  3.6 0.7 %all_to_all.9 = f32[8,1,4]{2,0,1:T(8,128)} reshape(f32[32]{0:T(128)S(1)} %scatter_custom_fusion) | data formatting | bytes 256 | tf_op jit(solution)/shard_map/all_to_all | solution.py:192
  4.3 6.4 %all-to-all-start = ((f32[8,1,4]{2,1,0:T(1,128)}), f32[8,1,4]{2,1,0:T(1,128)S(1)}, u32[]{:S(2)}, u32[]{:S(2)}) async-start(f32[8,1,4]{2,1,0:T(1,128)} %bitcast.104), calls=%async_computation | async-start | bytes 8192 | tf_op jit(solution)/shard_map/all_to_all | solution.py:192
  10.6 1.0 %pad_maximum_fusion.10 = f32[4,16,5,128]{3,1,0,2:T(8,128)S(1)} fusion(f32[4,16,1,128]{3,1,0,2:T(8,128)} %bitcast.1004, f32[4,16,1,128]{3,1,0,2:T(8,128)} %bitcast.1008, f32[4,16,3,128]{3,1,2,0:T(8,128)} %param.7), kind=kLoop, calls=%fused_computation.108 | loop fusion | flops 81920 | bytes 327680 | tf_op jit(solution)/shard_map/concatenate | solution.py:139
  11.7 1.5 %collective-permute-start = (f32[4,16,5,1]{3,1,0,2:T(8,128)S(1)}, f32[4,16,5,1]{3,1,0,2:T(8,128)S(1)}, u32[]{:S(2)}, u32[]{:S(2)}) collective-permute-start(f32[4,16,5,1]{3,1,0,2:T(8,128)S(1)} %get-tuple-element.108), channel_id=1, source_target_pairs={{0,4},{4,8},{8,12},{12,16},{16,20},{20,24},{24,28},{28,0},{1,5},{5... | collective-permute-start | bytes 3848 | tf_op jit(solution)/shard_map/ppermute | solution.py:30
  13.2 2.8 %collective-permute-start.1 = (f32[4,16,5,1]{3,1,0,2:T(8,128)S(1)}, f32[4,16,5,1]{3,1,0,2:T(8,128)S(1)}, u32[]{:S(2)}, u32[]{:S(2)}) collective-permute-start(f32[4,16,5,1]{3,1,0,2:T(8,128)S(1)} %get-tuple-element.109), channel_id=1, source_target_pairs={{4,0},{8,4},{12,8},{16,12},{20,16},{24,20},{28,24},{0,28},{5,1},{9... | collective-permute-start | bytes 3848 | tf_op jit(solution)/shard_map/ppermute | solution.py:32
  16.4 0.6 %gather_fusion.1 = f32[16,3,128]{2,1,0:T(4,128)S(1)} fusion(f32[64,3,128]{2,1,0:T(4,128)S(1)} %copy_add_fusion, s32[1024]{0:T(1024)S(1)} %pad_clamp_fusion), kind=kCustom, calls=%fused_computation.1 | custom fusion | bytes 49216 | tf_op jit(solution)/shard_map/gather | solution.py:177
  17.1 1.0 %scatter_fusion = f32[32,3,128]{2,1,0:T(4,128)S(1)} fusion(f32[32,3,128]{2,1,0:T(4,128)S(1)} %broadcast_in_dim.24, s32[16]{0:T(128)S(1)} %get-tuple-element.149, f32[16,3,128]{2,1,0:T(4,128)S(1)} %broadcast_subtract_fusion), kind=kCustom, calls=%fused_computation.3 | custom fusion | bytes 73792 | tf_op jit(solution)/shard_map/scatter | solution.py:177
  18.2 0.6 %copy.222 = f32[8,4,3,128]{3,1,2,0:T(4,128)} copy(f32[8,4,3,128]{3,2,1,0:T(4,128)S(1)} %bitcast.1018) | data formatting | bytes 98304 | tf_op jit(solution)/shard_map/reshape | solution.py:186
  18.8 3.3 %all-to-all-start.1 = ((f32[8,4,3,128]{3,1,2,0:T(4,128)}), f32[8,4,3,128]{3,1,2,0:T(4,128)S(1)}, u32[]{:S(2)}, u32[]{:S(2)}) async-start(f32[8,4,3,128]{3,1,2,0:T(4,128)} %copy.222), calls=%async_computation.1 | async-start | bytes 98304 | tf_op jit(solution)/shard_map/all_to_all | solution.py:185
  22.3 0.5 %broadcast.1172 = f32[]{:T(128)} broadcast(f32[]{:T(128)} %constant.1063), dimensions={} | broadcast | bytes 8 | tf_op jit(solution)/shard_map/all_to_all | solution.py:192
  22.8 0.7 %reduce.5 = f32[8,4]{1,0:T(8,128)S(1)} reduce(f32[8,1,4]{2,1,0:T(1,128)S(1)} %all-to-all-done, f32[]{:T(128)} %broadcast.1172), dimensions={1}, to_apply=%all_to_all.10.reduce_sub_computation.5 | reduce | bytes 260 | tf_op jit(solution)/shard_map/all_to_all | solution.py:192
  23.5 0.6 %gather_fusion = f32[32,3,128]{2,1,0:T(4,128)S(1)} fusion(f32[64,3,128]{2,1,0:T(4,128)S(1)} %copy_add_fusion, s32[1024]{0:T(1024)S(1)} %pad_clamp_fusion.1), kind=kCustom, calls=%fused_computation | custom fusion | bytes 98432 | tf_op jit(solution)/shard_map/gather | solution.py:200
  24.2 0.1 pad_maximum_fusion.72
  24.4 2.7 %collective-permute-start.2 = (f32[1,16,5,130]{3,1,0,2:T(8,128)S(1)}, f32[1,16,5,130]{3,1,0,2:T(8,128)S(1)}, u32[]{:S(2)}, u32[]{:S(2)}) collective-permute-start(f32[1,16,5,130]{3,1,0,2:T(8,128)S(1)} %get-tuple-element.106), channel_id=1, source_target_pairs={{0,1},{1,2},{2,3},{3,0},{4,5},{5,6},{6,7},{7,4},{8,9},{9,10},{10,1... | collective-permute-start | bytes 124808 | tf_op jit(solution)/shard_map/ppermute | solution.py:30
  27.0 1.5 %collective-permute-done.2 = f32[1,16,5,130]{3,1,0,2:T(8,128)S(1)} collective-permute-done((f32[1,16,5,130]{3,1,0,2:T(8,128)S(1)}, f32[1,16,5,130]{3,1,0,2:T(8,128)S(1)}, u32[]{:S(2)}, u32[]{:S(2)}) %collective-permute-start.2) | collective-permute-done | bytes 41632 | tf_op jit(solution)/shard_map/ppermute | solution.py:30
  28.5 2.4 %collective-permute-done.3 = f32[1,16,5,130]{3,1,0,2:T(8,128)S(1)} collective-permute-done((f32[1,16,5,130]{3,1,0,2:T(8,128)S(1)}, f32[1,16,5,130]{3,1,0,2:T(8,128)S(1)}, u32[]{:S(2)}, u32[]{:S(2)}) %collective-permute-start.3) | collective-permute-done | bytes 41632 | tf_op jit(solution)/shard_map/ppermute | solution.py:32
  30.9 0.1 pad_maximum_fusion.61
  31.1 0.1 fusion.187
  31.2 0.1 fusion.39
  31.4 0.1 fusion.186
  31.5 0.1 fusion.41
  31.6 0.1 fusion.10
  31.7 0.2 pad_maximum_fusion
  32.1 0.1 fusion.188
  32.2 0.1 fusion.44
  32.4 0.1 fusion.43
  32.5 0.1 slice_bitcast_fusion.41
  32.7 0.1 fusion.189
  32.8 0.1 fusion.40
  33.0 0.1 fusion.191
  33.1 0.1 fusion.42
  33.2 0.1 slice_bitcast_fusion.45
  33.3 1.2 %subtract_subtract_fusion.2 = (f32[6,16,130]{2,1,0:T(8,128)S(1)}, f32[6,16,130]{2,1,0:T(8,128)S(1)}, f32[6,16,130]{2,1,0:T(8,128)S(1)}, f32[6,16,130]{2,1,0:T(8,...) fusion(pred[130]{0:T(512)(128)(4,1)S(1)} %iota_compare_fusion.1, ...), kind=kLoop, calls=%fused_computation.403 | loop fusion | flops 2857920 | bytes 4043746 | tf_op jit(solution)/shard_map/sub | solution.py:106
  34.7 0.3 fusion.70
  35.0 0.3 subtract_add_fusion.3
  35.3 0.3 fusion.61
  35.6 0.3 subtract_add_fusion
  35.9 0.3 fusion.67
  36.2 0.3 fusion.58
  36.5 0.3 subtract_add_fusion.2
  36.7 0.3 subtract_add_fusion.5
  37.0 0.6 %subtract_subtract_fusion.1 = f32[6,16,130]{2,1,0:T(8,128)S(1)} fusion(f32[6,16,130]{2,1,0:T(8,128)S(1)} %get-tuple-element.97, f32[6,16,130]{2,1,0:T(8,128)S(1)} %get-tuple-element.99, f32[6,16,130]{2,1,0:T(8,128)S(1)} %get-tuple-element.98, f32[6,16,130]{2,1,0:T(8,128)S(1)} %get-tuple-element.87, f32[6,16,130]{2,1,0:T(8,128)S(1)} %get-tuple-element.85, ...), kind=kLoop, calls=%fused_computation.399 | loop fusion | flops 1235520 | bytes 2246626 | tf_op jit(solution)/shard_map/sub | solution.py:106
  37.6 0.6 %subtract_subtract_fusion = f32[6,16,130]{2,1,0:T(8,128)S(1)} fusion(f32[6,16,130]{2,1,0:T(8,128)S(1)} %get-tuple-element.89, f32[6,16,130]{2,1,0:T(8,128)S(1)} %get-tuple-element.85, f32[6,16,130]{2,1,0:T(8,128)S(1)} %get-tuple-element.95, f32[6,16,130]{2,1,0:T(8,128)S(1)} %get-tuple-element.98, f32[6,16,130]{2,1,0:T(8,128)S(1)} %get-tuple-element.90, ...), kind=kLoop, calls=%fused_computation.391 | loop fusion | flops 1235520 | bytes 2246626 | tf_op jit(solution)/shard_map/sub | solution.py:106
  38.2 0.3 fusion.64
  38.5 0.3 fusion.55
  38.8 0.3 subtract_add_fusion.4
  39.1 0.3 subtract_add_fusion.1
  39.7 0.6 %slice-done = f32[1,16,130]{2,1,0:T(8,128)S(1)} async-done(((f32[6,16,130]{2,1,0:T(8,128)}), f32[1,16,130]{2,1,0:T(8,128)S(1)}, s32[]{:S(2)}) %slice-start) | async-done | bytes 8344 | tf_op jit(solution)/shard_map/jit(_roll_static)/slice | solution.py:111
  40.2 0.2 slice-done.1
  41.2 0.2 fusion.52
  41.3 0.1 subtract_add_fusion.6
  41.5 0.1 fusion.49
  41.7 0.2 subtract_add_fusion.9
  41.8 0.1 fusion.46
  42.0 0.1 subtract_add_fusion.7
  42.6 1.0 %fusion.22 = (f32[6,16,1,130]{3,1,2,0:T(8,128)S(1)}, f32[6,16,1,130]{3,1,0,2:T(8,128)S(1)}, f32[6,16,1,130]{3,1,0,2:T(8,128)S(1)}, f32[6,16,1,130]{3,1,0,2:T(8,1...) fusion(f32[6,16,1,129]{3,1,0,2:T(8,128)S(1)} %slice_bitcast_fus, ...), kind=kLoop, calls=%fused_computation.138 | loop fusion | flops 2882880 | bytes 3045346 | tf_op jit(solution)/shard_map/add | solution.py:111
  43.6 0.8 %fusion.30 = f32[6,16,1,130]{3,1,2,0:T(8,128)S(1)} fusion(f32[6,16,1,129]{3,1,0,2:T(8,128)S(1)} %slice_bitcast_fusion.2, f32[6,16,1,1]{3,1,0,2:T(8,128)S(1)} %slice_bitcast_fusion.16, f32[6,15,1,130]{3,1,0,2:T(8,128)S(1)} %slice_bitcast_fusion.1, f32[6,1,1,130]{3,1,0,2:T(1,128)S(1)} %slice_bitcast_fusion.27, f32[6,16,1,129]{3,1,0,2:T(8,128)S(1)} %fusion.75, ...), kind=kLoop, calls=%fused_computation.146 | loop fusion | flops 2283840 | bytes 2446306 | tf_op jit(solution)/shard_map/add | solution.py:111
  44.5 0.8 %fusion.38 = f32[6,16,1,130]{3,1,2,0:T(8,128)S(1)} fusion(f32[6,16,1,129]{3,1,0,2:T(8,128)S(1)} %slice_bitcast_fusion.5, f32[6,16,1,1]{3,1,0,2:T(8,128)S(1)} %slice_bitcast_fusion.18, f32[6,15,1,130]{3,1,0,2:T(8,128)S(1)} %slice_bitcast_fusion.4, f32[6,1,1,130]{3,1,0,2:T(1,128)S(1)} %slice_bitcast_fusion.28, f32[6,16,1,129]{3,1,0,2:T(8,128)S(1)} %fusion.79, ...), kind=kLoop, calls=%fused_computation.154 | loop fusion | flops 2283840 | bytes 2446306 | tf_op jit(solution)/shard_map/add | solution.py:111
  45.4 3.8 %fusion.4 = (f32[32,128]{1,0:T(8,128)S(1)}, f32[32,128]{1,0:T(8,128)S(1)}, f32[32,128]{1,0:T(8,128)S(1)}) fusion(f32[32,128]{1,0:T(8,128)S(1)} %get-tuple-element.144, f32[32,128]{1,0:T(8,128)S(1)} %bitcast.1036, f32[32,128]{1,0:T(8,128)S(1)} %get-tuple-element.145, f32[32,128]{1,0:T(8,128)S(1)} %bitcast.1035, f32[32,128]{1,0:T(8,128)S(1)} %get-tuple-element.143, ...), kind=kLoop, calls=%fused_computation.14 | loop fusion | flops 7852032 | bytes 147456 | tf_op jit(solution)/shard_map/while/body/eval_jaxpr/reduce_sum | solution.py:120
  49.2 0.9 %multiply_add_fusion = (f32[4,16,3,128]{3,1,2,0:T(8,128)}, f32[4,16,3,128]{3,1,2,0:T(8,128)}) fusion(f32[4,16,3,128]{3,1,2,0:T(8,128)S(1)} %copy-done, f32[4,16,3,128]{3,1,2,0:T(8,128)S(1)} %copy-done.4, f32[32,1,128]{2,0,1:T(8,128)S(1)} %bitcast.1032, f32[32,1,128]{2,0,1:T(8,128)S(1)} %bitcast.1033, f32[32,1,128]{2,0,1:T(8,128)S(1)} %bitcast.1031, ...), kind=kOutput, calls=%fused_computation.390 | convolution fusion | flops 9650176 | bytes 592672 | tf_op jit(solution)/shard_map/kp,kcx->pcx/dot_general | solution.py:206
  (129 shorter events, 2.7 us)
Async XLA Ops:
  4.3 14.6 %all-to-all-start = ((f32[8,1,4]{2,1,0:T(1,128)}), f32[8,1,4]{2,1,0:T(1,128)S(1)}, u32[]{:S(2)}, u32[]{:S(2)}) async-start(f32[8,1,4]{2,1,0:T(1,128)} %bitcast.104), calls=%async_computation | async-start | bytes 8192 | tf_op jit(solution)/shard_map/all_to_all | solution.py:192
  10.6 5.4 %copy-start = (f32[4,16,3,128]{3,1,2,0:T(8,128)S(1)}, f32[4,16,3,128]{3,1,2,0:T(8,128)}, u32[]{:S(2)}) copy-start(f32[4,16,3,128]{3,1,2,0:T(8,128)} %param.7) | copy-start | bytes 294916
  11.6 4.5 %copy-start.5 = (f32[1,1,3,16]{3,1,2,0:T(1,128)S(1)}, f32[1,1,3,16]{3,1,2,0:T(1,128)}, u32[]{:S(2)}) copy-start(f32[1,1,3,16]{3,1,2,0:T(1,128)} %param.13) | copy-start | bytes 580
  11.7 12.5 %collective-permute-start = (f32[4,16,5,1]{3,1,0,2:T(8,128)S(1)}, f32[4,16,5,1]{3,1,0,2:T(8,128)S(1)}, u32[]{:S(2)}, u32[]{:S(2)}) collective-permute-start(f32[4,16,5,1]{3,1,0,2:T(8,128)S(1)} %get-tuple-element.108), channel_id=1, source_target_pairs={{0,4},{4,8},{8,12},{12,16},{16,20},{20,24},{24,28},{28,0},{1,5},{5... | collective-permute-start | bytes 3848 | tf_op jit(solution)/shard_map/ppermute | solution.py:30
  13.2 11.0 %collective-permute-start.1 = (f32[4,16,5,1]{3,1,0,2:T(8,128)S(1)}, f32[4,16,5,1]{3,1,0,2:T(8,128)S(1)}, u32[]{:S(2)}, u32[]{:S(2)}) collective-permute-start(f32[4,16,5,1]{3,1,0,2:T(8,128)S(1)} %get-tuple-element.109), channel_id=1, source_target_pairs={{4,0},{8,4},{12,8},{16,12},{20,16},{24,20},{28,24},{0,28},{5,1},{9... | collective-permute-start | bytes 3848 | tf_op jit(solution)/shard_map/ppermute | solution.py:32
  16.4 7.9 %copy-start.1 = (f32[4,16,128]{2,1,0:T(8,128)S(1)}, f32[4,16,128]{2,1,0:T(8,128)}, u32[]{:S(2)}) copy-start(f32[4,16,128]{2,1,0:T(8,128)} %param.10) | copy-start | bytes 98308
  16.4 7.9 %copy-start.2 = (f32[4,16,128]{2,1,0:T(8,128)S(1)}, f32[4,16,128]{2,1,0:T(8,128)}, u32[]{:S(2)}) copy-start(f32[4,16,128]{2,1,0:T(8,128)} %param.9) | copy-start | bytes 98308
  18.8 26.5 %all-to-all-start.1 = ((f32[8,4,3,128]{3,1,2,0:T(4,128)}), f32[8,4,3,128]{3,1,2,0:T(4,128)S(1)}, u32[]{:S(2)}, u32[]{:S(2)}) async-start(f32[8,4,3,128]{3,1,2,0:T(4,128)} %copy.222), calls=%async_computation.1 | async-start | bytes 98304 | tf_op jit(solution)/shard_map/all_to_all | solution.py:185
  24.4 4.2 %collective-permute-start.2 = (f32[1,16,5,130]{3,1,0,2:T(8,128)S(1)}, f32[1,16,5,130]{3,1,0,2:T(8,128)S(1)}, u32[]{:S(2)}, u32[]{:S(2)}) collective-permute-start(f32[1,16,5,130]{3,1,0,2:T(8,128)S(1)} %get-tuple-element.106), channel_id=1, source_target_pairs={{0,1},{1,2},{2,3},{3,0},{4,5},{5,6},{6,7},{7,4},{8,9},{9,10},{10,1... | collective-permute-start | bytes 124808 | tf_op jit(solution)/shard_map/ppermute | solution.py:30
  27.0 3.9 %collective-permute-start.3 = (f32[1,16,5,130]{3,1,0,2:T(8,128)S(1)}, f32[1,16,5,130]{3,1,0,2:T(8,128)S(1)}, u32[]{:S(2)}, u32[]{:S(2)}) collective-permute-start(f32[1,16,5,130]{3,1,0,2:T(8,128)S(1)} %get-tuple-element.107), channel_id=1, source_target_pairs={{1,0},{2,1},{3,2},{0,3},{5,4},{6,5},{7,6},{4,7},{9,8},{10,9},{11,1... | collective-permute-start | bytes 124808 | tf_op jit(solution)/shard_map/ppermute | solution.py:32
  38.2 1.3 %copy-start.3 = (f32[6,16,130]{2,1,0:T(8,128)}, f32[6,16,130]{2,1,0:T(8,128)S(1)}, u32[]{:S(2)}) copy-start(f32[6,16,130]{2,1,0:T(8,128)S(1)} %subtract_subtract_fusion) | copy-start | bytes 149764
  39.5 0.7 %slice-start = ((f32[6,16,130]{2,1,0:T(8,128)}), f32[1,16,130]{2,1,0:T(8,128)S(1)}, s32[]{:S(2)}) async-start(f32[6,16,130]{2,1,0:T(8,128)} %copy-done.3), calls=%async_computation.2 | async-start | bytes 32768 | tf_op jit(solution)/shard_map/jit(_roll_static)/slice | solution.py:111
  39.5 0.9 %slice-start.1 = ((f32[6,16,130]{2,1,0:T(8,128)}), f32[5,16,130]{2,1,0:T(8,128)S(1)}, s32[]{:S(2)}) async-start(f32[6,16,130]{2,1,0:T(8,128)} %copy-done.3), calls=%async_computation.3 | async-start | bytes 163840 | tf_op jit(solution)/shard_map/jit(_roll_static)/slice | solution.py:111
  45.4 3.8 %copy-start.4 = (f32[4,16,3,128]{3,1,2,0:T(8,128)S(1)}, f32[4,16,3,128]{3,1,2,0:T(8,128)}, u32[]{:S(2)}) copy-start(f32[4,16,3,128]{3,1,2,0:T(8,128)} %param.8) | copy-start | bytes 294916
where the time goes:
time: 50.5 us; the launch traced here: 50.1 us
  other arithmetic  19.6 us (39%)
  starting transfers between devices  16.7 us (33%)
  local copies, waits for them, and re-layouts  6.76 us (13%)
  waiting for transfers between devices  3.87 us (8%)
  between operations  2.34 us (5%)
  matrix products  0.94 us (2%)
    all_to_all x1, starting transfers between devices, local(): lax.all_to_all(labels.reshape(regions, CAP), 'region', split_axis=0, conc...  6.37 us
    ppermute x2, starting transfers between devices, with_halo(): lax.ppermute(tail, axis, [(i, (i + 1) % count) for i in range(count)])  4.18 us
    reduce_sum x1, other arithmetic, pair_forces(): jnp.sum(delta * kernel, axis=2)  3.82 us
    all_to_all x1, starting transfers between devices, local(): lax.all_to_all(outgoing.reshape(regions, CAP, 3, patch_len), 'region', sp...  3.35 us
    ppermute x2, starting transfers between devices, with_halo(): lax.ppermute(head, axis, [((i + 1) % count, i) for i in range(count)])  2.77 us
    add x3, other arithmetic, cell_forces(): summed = summed + jnp.roll(totals[offset][row], offset, axis=(0, 1, 2))  2.72 us
    sub x3, other arithmetic, cell_forces(): totals[summit][row] = totals[summit][row] - col_third  2.38 us
    ppermute x2, waiting for transfers between devices, with_halo(): lax.ppermute(head, axis, [((i + 1) % count, i) for i in range(count)])  2.38 us
  transfers between devices with their start and end apart: 6, of which 2 were waited for; matrix products, arithmetic and copies ran while one was open for 37% of the time, Pallas kernels for 0%

commit v1 on v0

--- a/solution.py
+++ b/solution.py
@@ -18,6 +18,18 @@
 )
 REST_VOLUME = 1.0 / 6.0
 STEP_TIME = 0.2
+
+
+def exchange_directly(value, axis, split, join):
+    ways, here = (lax.axis_size(axis), lax.axis_index(axis))
+    width = value.shape[split] // ways
+    turned = jnp.roll(value, -here * width, axis=split)
+    got = [lax.slice_in_dim(turned, 0, width, axis=split)]
+    for far in range(1, ways):
+        sent = lax.slice_in_dim(turned, far * width, (far + 1) * width, axis=split)
+        got.append(lax.ppermute(sent, axis, [(d, (d + far) % ways) for d in range(ways)]))
+    line = jnp.concatenate(got[::-1], axis=join)
+    return jnp.roll(line, (here + 1) * got[0].shape[join], axis=join)
 
 
 def with_halo(cells, sides, width):
@@ -182,13 +194,7 @@
         .set(peer_patch.astype(jnp.float32), mode="drop")
     )
     arrived, arrived_labels = (
-        lax.all_to_all(
-            outgoing.reshape(regions, CAP, 3, patch_len),
-            "region",
-            split_axis=0,
-            concat_axis=0,
-            tiled=True,
-        ),
+        exchange_directly(outgoing.reshape(regions, CAP, 3, patch_len), "region", 0, 0),
         lax.all_to_all(
             labels.reshape(regions, CAP), "region", split_axis=0, concat_axis=0, tiled=True
         ),

time: 50.5 us -> 63 us (1.25)
  the two profiles are of different devices: /device:TPU:1 before, /device:TPU:29 now
where the time goes in v1:
time: 63 us; the launch traced here: 62.7 us
  starting transfers between devices  21 us (33%)
  other arithmetic  19.8 us (31%)
  waiting for transfers between devices  12.2 us (19%)
  local copies, waits for them, and re-layouts  6.25 us (10%)
  between operations  2.42 us (4%)
  matrix products  0.93 us (1%)
    ppermute x7, waiting for transfers between devices, exchange_directly(): lax.ppermute(sent, axis, [(d, (d + far) % ways) for d in range(ways)])  12.2 us
    ppermute x2, starting transfers between devices, with_halo(): lax.ppermute(tail, axis, [(i, (i + 1) % count) for i in range(count)])  7.47 us
    ppermute x7, starting transfers between devices, exchange_directly(): lax.ppermute(sent, axis, [(d, (d + far) % ways) for d in range(ways)])  6.66 us
    all_to_all x1, starting transfers between devices, local(): lax.all_to_all(labels.reshape(regions, CAP), 'region', split_axis=0, conc...  5.44 us
    reduce_sum x1, other arithmetic, pair_forces(): jnp.sum(delta * kernel, axis=2)  4 us
    add x3, other arithmetic, cell_forces(): summed = summed + jnp.roll(totals[offset][row], offset, axis=(0, 1, 2))  2.72 us
    sub x3, other arithmetic, cell_forces(): totals[summit][row] = totals[summit][row] - col_third  2.38 us
    add x9, other arithmetic, cell_forces(): totals[upper][row] = totals[upper][row] + (col_third - col_second)  2.09 us
  transfers between devices with their start and end apart: 12, of which 3 were waited for; matrix products, arithmetic and copies ran while one was open for 15% of the time, Pallas kernels for 0%

profile of v1, /device:TPU:29, one launch (start us, length us, event | category | flops | bytes accessed | tf_op | source)
XLA Modules:
  0.0 62.7 jit_solution(17779454078139347466)
XLA Ops:
  1.3 0.7 %convert_bitcast_fusion = (f32[16]{0:T(128)S(1)}, s32[16]{0:T(128)S(1)}) fusion(s32[1,1,3,16]{3,1,2,0:T(1,128)} %param.13), kind=kLoop, calls=%fused_computation.637 | loop fusion | flops 16 | bytes 256 | tf_op jit(solution)/shard_map/convert_element_type | solution.py:194
  2.1 0.2 select_reduce_fusion
  2.3 0.7 %fusion.165 = (s32[16]{0:T(128)S(1)}, s32[16]{0:T(128)S(1)}) fusion(s32[1,1,3,16]{3,1,2,0:T(1,128)} %param.13, s32[16]{0:T(128)S(1)} %select_reduce_fusion, s32[]{:T(128)} %bitcast.952), kind=kLoop, calls=%fused_computation.632 | loop fusion | flops 160 | bytes 324 | tf_op jit(solution)/shard_map/select_n | solution.py:189
  2.9 0.6 scatter_custom_fusion
  3.6 0.7 %all_to_all.6 = f32[8,1,4]{2,0,1:T(8,128)} reshape(f32[32]{0:T(128)S(1)} %scatter_custom_fusion) | data formatting | bytes 256 | tf_op jit(solution)/shard_map/all_to_all | solution.py:198
  4.3 5.4 %all-to-all-start = ((f32[8,1,4]{2,1,0:T(1,128)}), f32[8,1,4]{2,1,0:T(1,128)S(1)}, u32[]{:S(2)}, u32[]{:S(2)}) async-start(f32[8,1,4]{2,1,0:T(1,128)} %bitcast.104), calls=%async_computation | async-start | bytes 8192 | tf_op jit(solution)/shard_map/all_to_all | solution.py:198
  9.7 1.0 %pad_maximum_fusion.10 = f32[4,16,5,128]{3,1,0,2:T(8,128)S(1)} fusion(f32[4,16,1,128]{3,1,0,2:T(8,128)} %bitcast.1004, f32[4,16,1,128]{3,1,0,2:T(8,128)} %bitcast.1008, f32[4,16,3,128]{3,1,2,0:T(8,128)} %param.9), kind=kLoop, calls=%fused_computation.108 | loop fusion | flops 81920 | bytes 327680 | tf_op jit(solution)/shard_map/concatenate | solution.py:151
  10.9 1.5 %collective-permute-start.1 = (f32[4,16,5,1]{3,1,0,2:T(8,128)S(1)}, f32[4,16,5,1]{3,1,0,2:T(8,128)S(1)}, u32[]{:S(2)}, u32[]{:S(2)}) collective-permute-start(f32[4,16,5,1]{3,1,0,2:T(8,128)S(1)} %get-tuple-element.110), channel_id=1, source_target_pairs={{4,0},{8,4},{12,8},{16,12},{20,16},{24,20},{28,24},{0,28},{5,1},{9... | collective-permute-start | bytes 3848 | tf_op jit(solution)/shard_map/ppermute | solution.py:44
  12.9 0.5 broadcast.1173
  13.4 0.7 %reduce.5 = f32[8,4]{1,0:T(8,128)S(1)} reduce(f32[8,1,4]{2,1,0:T(1,128)S(1)} %all-to-all-done, f32[]{:T(128)} %broadcast.1173), dimensions={1}, to_apply=%all_to_all.7.reduce_sub_computation.5 | reduce | bytes 260 | tf_op jit(solution)/shard_map/all_to_all | solution.py:198
  14.1 0.6 gather_fusion.1
  14.7 0.6 gather_fusion
  15.5 1.0 %scatter_fusion = f32[32,3,128]{2,1,0:T(4,128)S(1)} fusion(f32[32,3,128]{2,1,0:T(4,128)S(1)} %broadcast_in_dim.24, s32[16]{0:T(128)S(1)} %get-tuple-element.157, f32[16,3,128]{2,1,0:T(4,128)S(1)} %broadcast_subtract_fusion), kind=kCustom, calls=%fused_computation.3 | custom fusion | bytes 73792 | tf_op jit(solution)/shard_map/scatter | solution.py:189
  16.6 2.8 %collective-permute-start.10 = (f32[1,4,3,128]{3,1,0,2:T(4,128)S(1)}, f32[1,4,3,128]{3,1,0,2:T(4,128)S(1)}, u32[]{:S(2)}, u32[]{:S(2)}) collective-permute-start(f32[1,4,3,128]{3,1,0,2:T(4,128)S(1)} %get-tuple-element.147), channel_id=1, source_target_pairs={{0,4},{4,8},{8,12},{12,16},{16,20},{20,24},{24,28},{28,0},{1,5},{5... | collective-permute-start | bytes 18440 | tf_op jit(solution)/shard_map/ppermute | solution.py:30
  19.5 2.4 %collective-permute-start.7 = (f32[1,4,3,128]{3,1,0,2:T(4,128)S(1)}, f32[1,4,3,128]{3,1,0,2:T(4,128)S(1)}, u32[]{:S(2)}, u32[]{:S(2)}) collective-permute-start(f32[1,4,3,128]{3,1,0,2:T(4,128)S(1)} %get-tuple-element.150), channel_id=1, source_target_pairs={{0,16},{4,20},{8,24},{12,28},{16,0},{20,4},{24,8},{28,12},{1,17},{... | collective-permute-start | bytes 18440 | tf_op jit(solution)/shard_map/ppermute | solution.py:30
  21.9 1.4 %collective-permute-start.4 = (f32[1,4,3,128]{3,1,0,2:T(4,128)S(1)}, f32[1,4,3,128]{3,1,0,2:T(4,128)S(1)}, u32[]{:S(2)}, u32[]{:S(2)}) collective-permute-start(f32[1,4,3,128]{3,1,0,2:T(4,128)S(1)} %get-tuple-element.153), channel_id=1, source_target_pairs={{0,28},{4,0},{8,4},{12,8},{16,12},{20,16},{24,20},{28,24},{1,29},{... | collective-permute-start | bytes 18440 | tf_op jit(solution)/shard_map/ppermute | solution.py:30
  23.3 0.1 pad_maximum_fusion.72
  23.4 3.6 %collective-permute-done.4 = f32[1,4,3,128]{3,1,0,2:T(4,128)S(1)} collective-permute-done((f32[1,4,3,128]{3,1,0,2:T(4,128)S(1)}, f32[1,4,3,128]{3,1,0,2:T(4,128)S(1)}, u32[]{:S(2)}, u32[]{:S(2)}) %collective-permute-start.4) | collective-permute-done | bytes 6176 | tf_op jit(solution)/shard_map/ppermute | solution.py:30
  27.1 4.3 %collective-permute-done.5 = f32[1,4,3,128]{3,1,0,2:T(4,128)S(1)} collective-permute-done((f32[1,4,3,128]{3,1,0,2:T(4,128)S(1)}, f32[1,4,3,128]{3,1,0,2:T(4,128)S(1)}, u32[]{:S(2)}, u32[]{:S(2)}) %collective-permute-start.5) | collective-permute-done | bytes 6176 | tf_op jit(solution)/shard_map/ppermute | solution.py:30
  31.4 4.3 %collective-permute-done.6 = f32[1,4,3,128]{3,1,0,2:T(4,128)S(1)} collective-permute-done((f32[1,4,3,128]{3,1,0,2:T(4,128)S(1)}, f32[1,4,3,128]{3,1,0,2:T(4,128)S(1)}, u32[]{:S(2)}, u32[]{:S(2)}) %collective-permute-start.6) | collective-permute-done | bytes 6176 | tf_op jit(solution)/shard_map/ppermute | solution.py:30
  35.6 7.4 %collective-permute-start.2 = (f32[1,16,5,130]{3,1,0,2:T(8,128)S(1)}, f32[1,16,5,130]{3,1,0,2:T(8,128)S(1)}, u32[]{:S(2)}, u32[]{:S(2)}) collective-permute-start(f32[1,16,5,130]{3,1,0,2:T(8,128)S(1)} %get-tuple-element.107), channel_id=1, source_target_pairs={{0,1},{1,2},{2,3},{3,0},{4,5},{5,6},{6,7},{7,4},{8,9},{9,10},{10,1... | collective-permute-start | bytes 124808 | tf_op jit(solution)/shard_map/ppermute | solution.py:42
  43.2 4.0 %fusion.4 = (f32[32,128]{1,0:T(8,128)S(1)}, f32[32,128]{1,0:T(8,128)S(1)}, f32[32,128]{1,0:T(8,128)S(1)}) fusion(f32[32,128]{1,0:T(8,128)S(1)} %get-tuple-element.145, f32[32,128]{1,0:T(8,128)S(1)} %bitcast.1036, f32[32,128]{1,0:T(8,128)S(1)} %get-tuple-element.146, f32[32,128]{1,0:T(8,128)S(1)} %bitcast.1035, f32[32,128]{1,0:T(8,128)S(1)} %get-tuple-element.144, ...), kind=kLoop, calls=%fused_computation.14 | loop fusion | flops 7852032 | bytes 147456 | tf_op jit(solution)/shard_map/while/body/eval_jaxpr/reduce_sum | solution.py:132
  47.3 0.1 pad_maximum_fusion.61
  47.6 0.1 fusion.39
  47.7 0.1 fusion.189
  47.8 0.1 fusion.41
  48.0 0.1 fusion.10
  48.1 0.2 pad_maximum_fusion
  48.4 0.1 fusion.191
  48.6 0.1 fusion.44
  48.8 0.1 fusion.43
  48.9 0.1 slice_bitcast_fusion.41
  49.1 0.1 fusion.192
  49.2 0.1 fusion.40
  49.3 0.1 fusion.194
  49.4 0.1 fusion.42
  49.5 0.1 slice_bitcast_fusion.45
  49.7 1.2 %subtract_subtract_fusion.2 = (f32[6,16,130]{2,1,0:T(8,128)S(1)}, f32[6,16,130]{2,1,0:T(8,128)S(1)}, f32[6,16,130]{2,1,0:T(8,128)S(1)}, f32[6,16,130]{2,1,0:T(8,...) fusion(pred[130]{0:T(512)(128)(4,1)S(1)} %iota_compare_fusion.1, ...), kind=kLoop, calls=%fused_computation.407 | loop fusion | flops 2857920 | bytes 4043746 | tf_op jit(solution)/shard_map/sub | solution.py:118
  51.0 0.3 fusion.70
  51.3 0.3 subtract_add_fusion.3
  51.7 0.3 fusion.61
  52.0 0.3 subtract_add_fusion
  52.3 0.3 fusion.67
  52.5 0.3 fusion.58
  52.8 0.3 subtract_add_fusion.2
  53.1 0.3 subtract_add_fusion.5
  53.4 0.6 subtract_subtract_fusion.1
  54.0 0.6 subtract_subtract_fusion
  54.6 0.3 fusion.64
  54.9 0.3 fusion.55
  55.1 0.3 subtract_add_fusion.4
  55.4 0.3 subtract_add_fusion.1
  56.0 0.6 slice-done
  56.6 0.2 slice-done.1
  57.5 0.2 fusion.52
  57.7 0.1 subtract_add_fusion.6
  57.9 0.1 fusion.49
  58.0 0.2 subtract_add_fusion.9
  58.2 0.1 fusion.46
  58.3 0.1 subtract_add_fusion.7
  58.9 1.0 %fusion.22 = (f32[6,16,1,130]{3,1,2,0:T(8,128)S(1)}, f32[6,16,1,130]{3,1,0,2:T(8,128)S(1)}, f32[6,16,1,130]{3,1,0,2:T(8,128)S(1)}, f32[6,16,1,130]{3,1,0,2:T(8,1...) fusion(f32[6,16,1,129]{3,1,0,2:T(8,128)S(1)} %slice_bitcast_fus, ...), kind=kLoop, calls=%fused_computation.138 | loop fusion | flops 2882880 | bytes 3045346 | tf_op jit(solution)/shard_map/add | solution.py:123
  60.0 0.8 %fusion.30 = f32[6,16,1,130]{3,1,2,0:T(8,128)S(1)} fusion(f32[6,16,1,129]{3,1,0,2:T(8,128)S(1)} %slice_bitcast_fusion.2, f32[6,16,1,1]{3,1,0,2:T(8,128)S(1)} %slice_bitcast_fusion.16, f32[6,15,1,130]{3,1,0,2:T(8,128)S(1)} %slice_bitcast_fusion.1, f32[6,1,1,130]{3,1,0,2:T(1,128)S(1)} %slice_bitcast_fusion.27, f32[6,16,1,129]{3,1,0,2:T(8,128)S(1)} %fusion.75, ...), kind=kLoop, calls=%fused_computation.146 | loop fusion | flops 2283840 | bytes 2446306 | tf_op jit(solution)/shard_map/add | solution.py:123
  60.8 0.8 %fusion.38 = f32[6,16,1,130]{3,1,2,0:T(8,128)S(1)} fusion(f32[6,16,1,129]{3,1,0,2:T(8,128)S(1)} %slice_bitcast_fusion.5, f32[6,16,1,1]{3,1,0,2:T(8,128)S(1)} %slice_bitcast_fusion.18, f32[6,15,1,130]{3,1,0,2:T(8,128)S(1)} %slice_bitcast_fusion.4, f32[6,1,1,130]{3,1,0,2:T(1,128)S(1)} %slice_bitcast_fusion.28, f32[6,16,1,129]{3,1,0,2:T(8,128)S(1)} %fusion.79, ...), kind=kLoop, calls=%fused_computation.154 | loop fusion | flops 2283840 | bytes 2446306 | tf_op jit(solution)/shard_map/add | solution.py:123
  61.7 0.9 %multiply_add_fusion = (f32[4,16,3,128]{3,1,2,0:T(8,128)}, f32[4,16,3,128]{3,1,2,0:T(8,128)}) fusion(f32[4,16,3,128]{3,1,2,0:T(8,128)S(1)} %copy-done, f32[4,16,3,128]{3,1,2,0:T(8,128)S(1)} %copy-done.4, f32[32,1,128]{2,0,1:T(8,128)S(1)} %bitcast.1032, f32[32,1,128]{2,0,1:T(8,128)S(1)} %bitcast.1033, f32[32,1,128]{2,0,1:T(8,128)S(1)} %bitcast.1031, ...), kind=kOutput, calls=%fused_computation.394 | convolution fusion | flops 9650176 | bytes 592672 | tf_op jit(solution)/shard_map/kp,kcx->pcx/dot_general | solution.py:212
  (150 shorter events, 3.1 us)
Async XLA Ops:
  4.3 8.5 %all-to-all-start = ((f32[8,1,4]{2,1,0:T(1,128)}), f32[8,1,4]{2,1,0:T(1,128)S(1)}, u32[]{:S(2)}, u32[]{:S(2)}) async-start(f32[8,1,4]{2,1,0:T(1,128)} %bitcast.104), calls=%async_computation | async-start | bytes 8192 | tf_op jit(solution)/shard_map/all_to_all | solution.py:198
  9.7 2.7 %copy-start = (f32[4,16,3,128]{3,1,2,0:T(8,128)S(1)}, f32[4,16,3,128]{3,1,2,0:T(8,128)}, u32[]{:S(2)}) copy-start(f32[4,16,3,128]{3,1,2,0:T(8,128)} %param.9) | copy-start | bytes 294916
  10.7 1.7 %copy-start.5 = (f32[1,1,3,16]{3,1,2,0:T(1,128)S(1)}, f32[1,1,3,16]{3,1,2,0:T(1,128)}, u32[]{:S(2)}) copy-start(f32[1,1,3,16]{3,1,2,0:T(1,128)} %param.15) | copy-start | bytes 580
  10.8 8.7 %collective-permute-start = (f32[4,16,5,1]{3,1,0,2:T(8,128)S(1)}, f32[4,16,5,1]{3,1,0,2:T(8,128)S(1)}, u32[]{:S(2)}, u32[]{:S(2)}) collective-permute-start(f32[4,16,5,1]{3,1,0,2:T(8,128)S(1)} %get-tuple-element.109), channel_id=1, source_target_pairs={{0,4},{4,8},{8,12},{12,16},{16,20},{20,24},{24,28},{28,0},{1,5},{5... | collective-permute-start | bytes 3848 | tf_op jit(solution)/shard_map/ppermute | solution.py:42
  10.9 11.0 %collective-permute-start.1 = (f32[4,16,5,1]{3,1,0,2:T(8,128)S(1)}, f32[4,16,5,1]{3,1,0,2:T(8,128)S(1)}, u32[]{:S(2)}, u32[]{:S(2)}) collective-permute-start(f32[4,16,5,1]{3,1,0,2:T(8,128)S(1)} %get-tuple-element.110), channel_id=1, source_target_pairs={{4,0},{8,4},{12,8},{16,12},{20,16},{24,20},{28,24},{0,28},{5,1},{9... | collective-permute-start | bytes 3848 | tf_op jit(solution)/shard_map/ppermute | solution.py:44
  12.7 10.6 %copy-start.1 = (f32[4,16,128]{2,1,0:T(8,128)S(1)}, f32[4,16,128]{2,1,0:T(8,128)}, u32[]{:S(2)}) copy-start(f32[4,16,128]{2,1,0:T(8,128)} %param.12) | copy-start | bytes 98308
  12.7 10.6 %copy-start.2 = (f32[4,16,128]{2,1,0:T(8,128)S(1)}, f32[4,16,128]{2,1,0:T(8,128)}, u32[]{:S(2)}) copy-start(f32[4,16,128]{2,1,0:T(8,128)} %param.11) | copy-start | bytes 98308
  16.6 26.5 %collective-permute-start.10 = (f32[1,4,3,128]{3,1,0,2:T(4,128)S(1)}, f32[1,4,3,128]{3,1,0,2:T(4,128)S(1)}, u32[]{:S(2)}, u32[]{:S(2)}) collective-permute-start(f32[1,4,3,128]{3,1,0,2:T(4,128)S(1)} %get-tuple-element.147), channel_id=1, source_target_pairs={{0,4},{4,8},{8,12},{12,16},{16,20},{20,24},{24,28},{28,0},{1,5},{5... | collective-permute-start | bytes 18440 | tf_op jit(solution)/shard_map/ppermute | solution.py:30
  19.4 23.6 %collective-permute-start.9 = (f32[1,4,3,128]{3,1,0,2:T(4,128)S(1)}, f32[1,4,3,128]{3,1,0,2:T(4,128)S(1)}, u32[]{:S(2)}, u32[]{:S(2)}) collective-permute-start(f32[1,4,3,128]{3,1,0,2:T(4,128)S(1)} %get-tuple-element.148), channel_id=1, source_target_pairs={{0,8},{4,12},{8,16},{12,20},{16,24},{20,28},{24,0},{28,4},{1,9},{5... | collective-permute-start | bytes 18440 | tf_op jit(solution)/shard_map/ppermute | solution.py:30
  19.4 23.6 %collective-permute-start.8 = (f32[1,4,3,128]{3,1,0,2:T(4,128)S(1)}, f32[1,4,3,128]{3,1,0,2:T(4,128)S(1)}, u32[]{:S(2)}, u32[]{:S(2)}) collective-permute-start(f32[1,4,3,128]{3,1,0,2:T(4,128)S(1)} %get-tuple-element.149), channel_id=1, source_target_pairs={{0,12},{4,16},{8,20},{12,24},{16,28},{20,0},{24,4},{28,8},{1,13},{... | collective-permute-start | bytes 18440 | tf_op jit(solution)/shard_map/ppermute | solution.py:30
  19.5 23.6 %collective-permute-start.7 = (f32[1,4,3,128]{3,1,0,2:T(4,128)S(1)}, f32[1,4,3,128]{3,1,0,2:T(4,128)S(1)}, u32[]{:S(2)}, u32[]{:S(2)}) collective-permute-start(f32[1,4,3,128]{3,1,0,2:T(4,128)S(1)} %get-tuple-element.150), channel_id=1, source_target_pairs={{0,16},{4,20},{8,24},{12,28},{16,0},{20,4},{24,8},{28,12},{1,17},{... | collective-permute-start | bytes 18440 | tf_op jit(solution)/shard_map/ppermute | solution.py:30
  21.9 5.2 %collective-permute-start.4 = (f32[1,4,3,128]{3,1,0,2:T(4,128)S(1)}, f32[1,4,3,128]{3,1,0,2:T(4,128)S(1)}, u32[]{:S(2)}, u32[]{:S(2)}) collective-permute-start(f32[1,4,3,128]{3,1,0,2:T(4,128)S(1)} %get-tuple-element.153), channel_id=1, source_target_pairs={{0,28},{4,0},{8,4},{12,8},{16,12},{20,16},{24,20},{28,24},{1,29},{... | collective-permute-start | bytes 18440 | tf_op jit(solution)/shard_map/ppermute | solution.py:30
  27.1 4.3 %collective-permute-start.5 = (f32[1,4,3,128]{3,1,0,2:T(4,128)S(1)}, f32[1,4,3,128]{3,1,0,2:T(4,128)S(1)}, u32[]{:S(2)}, u32[]{:S(2)}) collective-permute-start(f32[1,4,3,128]{3,1,0,2:T(4,128)S(1)} %get-tuple-element.152), channel_id=1, source_target_pairs={{0,24},{4,28},{8,0},{12,4},{16,8},{20,12},{24,16},{28,20},{1,25},{... | collective-permute-start | bytes 18440 | tf_op jit(solution)/shard_map/ppermute | solution.py:30
  31.3 4.3 %collective-permute-start.6 = (f32[1,4,3,128]{3,1,0,2:T(4,128)S(1)}, f32[1,4,3,128]{3,1,0,2:T(4,128)S(1)}, u32[]{:S(2)}, u32[]{:S(2)}) collective-permute-start(f32[1,4,3,128]{3,1,0,2:T(4,128)S(1)} %get-tuple-element.151), channel_id=1, source_target_pairs={{0,20},{4,24},{8,28},{12,0},{16,4},{20,8},{24,12},{28,16},{1,21},{... | collective-permute-start | bytes 18440 | tf_op jit(solution)/shard_map/ppermute | solution.py:30
  35.6 11.6 %collective-permute-start.2 = (f32[1,16,5,130]{3,1,0,2:T(8,128)S(1)}, f32[1,16,5,130]{3,1,0,2:T(8,128)S(1)}, u32[]{:S(2)}, u32[]{:S(2)}) collective-permute-start(f32[1,16,5,130]{3,1,0,2:T(8,128)S(1)} %get-tuple-element.107), channel_id=1, source_target_pairs={{0,1},{1,2},{2,3},{3,0},{4,5},{5,6},{6,7},{7,4},{8,9},{9,10},{10,1... | collective-permute-start | bytes 124808 | tf_op jit(solution)/shard_map/ppermute | solution.py:42
  43.0 4.2 %collective-permute-start.3 = (f32[1,16,5,130]{3,1,0,2:T(8,128)S(1)}, f32[1,16,5,130]{3,1,0,2:T(8,128)S(1)}, u32[]{:S(2)}, u32[]{:S(2)}) collective-permute-start(f32[1,16,5,130]{3,1,0,2:T(8,128)S(1)} %get-tuple-element.108), channel_id=1, source_target_pairs={{1,0},{2,1},{3,2},{0,3},{5,4},{6,5},{7,6},{4,7},{9,8},{10,9},{11,1... | collective-permute-start | bytes 124808 | tf_op jit(solution)/shard_map/ppermute | solution.py:44
  54.6 1.3 %copy-start.3 = (f32[6,16,130]{2,1,0:T(8,128)}, f32[6,16,130]{2,1,0:T(8,128)S(1)}, u32[]{:S(2)}) copy-start(f32[6,16,130]{2,1,0:T(8,128)S(1)} %subtract_subtract_fusion) | copy-start | bytes 149764
  55.9 0.7 %slice-start = ((f32[6,16,130]{2,1,0:T(8,128)}), f32[1,16,130]{2,1,0:T(8,128)S(1)}, s32[]{:S(2)}) async-start(f32[6,16,130]{2,1,0:T(8,128)} %copy-done.3), calls=%async_computation.1 | async-start | bytes 32768 | tf_op jit(solution)/shard_map/jit(_roll_static)/slice | solution.py:123
  55.9 0.9 %slice-start.1 = ((f32[6,16,130]{2,1,0:T(8,128)}), f32[5,16,130]{2,1,0:T(8,128)S(1)}, s32[]{:S(2)}) async-start(f32[6,16,130]{2,1,0:T(8,128)} %copy-done.3), calls=%async_computation.2 | async-start | bytes 163840 | tf_op jit(solution)/shard_map/jit(_roll_static)/slice | solution.py:123
  60.8 0.9 %copy-start.4 = (f32[4,16,3,128]{3,1,2,0:T(8,128)S(1)}, f32[4,16,3,128]{3,1,2,0:T(8,128)}, u32[]{:S(2)}) copy-start(f32[4,16,3,128]{3,1,2,0:T(8,128)} %param.10) | copy-start | bytes 294916
